TPU v7x, 32 devices: a whole 2x2x4 slice. The times are simulated.
32 devices in a mesh: row: 2 (over x), col: 16 (over z, y, core).
Axes of the slice: x: 2, y: 2, z: 4, core: 2. Of those that a mesh axis runs over, the one named last changes fastest.
Arguments:
- diagonal_tile: float32 [512, 512], P('row'), may hold values from -1 to 8, as said below
- panel: float32 [2048, 512], P(('row', 'col')), may hold values from -2.5 to 2.5
- trailing: bfloat16 [2048, 2048], P('col', 'row'), may hold values from -6 to 6
Outputs:
- factor_panel: float32 [2048, 512], P(('row', 'col'))
- updated: bfloat16 [2048, 2048], P('col', 'row')
Inputs may be any that keep to these rules, and one draw needn't show every extreme that they name: `diagonal_tile`: symmetric, and every eigenvalue is at least 1.
All inputs are finite; a program needn't handle non-finite values.
Results may differ from a plain program's by a relative error of at most 0.0085.
Values may be sent and summed in bfloat16 or wider, within the bound.
A program may use at most 64 MiB of HBM per device.

v0:
```python
import jax
import jax.numpy as jnp
from jax import lax
from jax.sharding import PartitionSpec as P


def per_device(diagonal_tile, panel, trailing):
    tile_whole = lax.all_gather(diagonal_tile, "row", axis=0, tiled=True)
    diag_factor = jnp.linalg.cholesky(tile_whole)

    def solve_rows(panel_rows):
        return jax.scipy.linalg.solve_triangular(diag_factor, panel_rows.T, lower=True).T

    factor_panel = solve_rows(panel)
    low_panel = factor_panel.astype(jnp.bfloat16)
    raw_rows = lax.all_gather(panel.astype(jnp.bfloat16), "row", axis=0, tiled=True).astype(
        panel.dtype
    )
    column_low = solve_rows(raw_rows).astype(jnp.bfloat16)
    block_low = lax.all_gather(low_panel, "col", axis=0, tiled=True)
    outer_term = lax.dot_general(
        column_low, block_low, (((1,), (1,)), ((), ())), preferred_element_type=jnp.float32
    )
    updated = (trailing.astype(jnp.float32) - outer_term).astype(jnp.bfloat16)
    return (factor_panel, updated)


def solution(mesh):
    return jax.shard_map(
        per_device,
        mesh=mesh,
        in_specs=(P("row", None), P(("row", "col"), None), P("col", "row")),
        out_specs=(P(("row", "col"), None), P("col", "row")),
        check_vma=False,
    )
```

profile of v0, /device:TPU:0, one launch (start us, length us, event | category | flops | bytes accessed | tf_op | source)
XLA Modules:
  0.0 216.5 jit_solution(180372973036767981)
XLA Ops:
  7.2 2.1 copy.5
  9.4 24.2 %all-gather.3.cloned.1.call-done = f32[512,512]{0,1:T(8,128)} async-done(((f32[256,512]{0,1:T(8,128)}), f32[512,512]{0,1:T(8,128)}) %all-gather.3.cloned.1.call-update) | async-done | bytes 1048592 | tf_op jit(solution)/shard_map/all_gather | solution.py:8
  33.6 1.6 copy.6
  35.5 11.7 %cholesky.104 = f32[128,128]{1,0:T(8,128)S(1)} custom-call(f32[128,128]{1,0:T(8,128)S(1)} %cholesky.266), custom_call_target="Cholesky" | custom-call | tf_op jit(solution)/shard_map/jit(cholesky)/cholesky | solution.py:9
  47.2 9.8 %custom-call.34 = f32[1,128,128]{1,2,0:T(8,128)S(1)} custom-call(f32[1,128,128]{2,1,0:T(8,128)S(1)} %get-tuple-element.31), custom_call_target="InvertDiagBlocksLowerTriangular" | custom-call | tf_op jit(solution)/shard_map/jit(cholesky)/cholesky | solution.py:9
  57.8 11.7 %cholesky.217 = f32[128,128]{1,0:T(8,128)S(1)} custom-call(f32[128,128]{1,0:T(8,128)S(1)} %cholesky.270), custom_call_target="Cholesky" | custom-call | tf_op jit(solution)/shard_map/jit(cholesky)/cholesky | solution.py:9
  69.6 10.0 %custom-call.35 = f32[1,128,128]{1,2,0:T(8,128)S(1)} custom-call(f32[1,128,128]{2,1,0:T(8,128)S(1)} %get-tuple-element.28), custom_call_target="InvertDiagBlocksLowerTriangular" | custom-call | tf_op jit(solution)/shard_map/jit(cholesky)/cholesky | solution.py:9
  79.8 0.4 convolution_subtract_fusion.2
  80.2 11.7 %cholesky.238 = f32[128,128]{1,0:T(8,128)S(1)} custom-call(f32[128,128]{1,0:T(8,128)S(1)} %cholesky.275), custom_call_target="Cholesky" | custom-call | tf_op jit(solution)/shard_map/jit(cholesky)/cholesky | solution.py:9
  92.0 0.7 compare_reduce_fusion.1
  92.7 9.8 %custom-call.36 = f32[1,128,128]{1,2,0:T(8,128)S(1)} custom-call(f32[1,128,128]{2,1,0:T(8,128)S(1)} %get-tuple-element.25), custom_call_target="InvertDiagBlocksLowerTriangular" | custom-call | tf_op jit(solution)/shard_map/jit(cholesky)/cholesky | solution.py:9
  102.7 0.4 convolution_subtract_fusion.6
  103.1 11.7 %cholesky.255 = f32[128,128]{1,0:T(8,128)S(1)} custom-call(f32[128,128]{1,0:T(8,128)S(1)} %convolution_subtract_fusion.6), custom_call_target="Cholesky" | custom-call | tf_op jit(solution)/shard_map/jit(cholesky)/cholesky | solution.py:9
  114.8 0.6 compare_reduce_fusion
  115.5 0.7 compare_reduce_fusion.2
  119.0 8.5 %while.1 = (s32[]{:T(128)}, f32[512,512]{1,0:T(8,128)S(1)}, s32[4,2]{0,1:T(2,128)S(1)}, f32[4,128,128]{2,1,0:T(8,128)S(1)}, s32[]{:T(128)}) while((s32[]{:T(128)}, f32[512,512]{1,0:T(8,128)S(1)}, s32[4,2]{0,1:T(2,128)S(1)}, f32[4,128,128]{2,1,0:T(8,128)S(1)}, s32[]{:T(128)}) %tuple.35), condition=%wide.while_cond, body=%wide.while_body.sunk | while | flops 2 | bytes 131181 | solution.py:12
  119.1 0.6 fusion.72
  119.7 1.4 bitcast_dynamic-update-slice_fusion.2
  121.3 0.6 fusion.72
  121.9 1.4 bitcast_dynamic-update-slice_fusion.2
  123.4 0.6 fusion.72
  124.0 1.4 bitcast_dynamic-update-slice_fusion.2
  125.5 0.6 fusion.72
  126.1 1.4 bitcast_dynamic-update-slice_fusion.2
  127.5 39.3 %custom-call.37 = f32[4,128,128]{1,2,0:T(8,128)S(1)} custom-call(f32[4,128,128]{2,1,0:T(8,128)S(1)} %get-tuple-element.9), custom_call_target="InvertDiagBlocksLowerTriangular" | custom-call | tf_op jit(solution)/shard_map/jit(_solve_triangular)/triangular_solve | solution.py:12
  168.0 0.4 convolution_subtract_fusion.7
  168.6 0.7 fusion.56
  169.3 4.9 %all_gather.10 = bf16[128,512]{1,0:T(8,128)(2,1)S(1)} all-gather(bf16[64,512]{1,0:T(8,128)(2,1)S(1)} %convert_element_type.16), channel_id=1, replica_groups=mesh['row'=2,'col'=16] {'row'}, dimensions={0}, use_global_device_ids=true | all-gather | bytes 196608 | tf_op jit(solution)/shard_map/all_gather | solution.py:16
  175.1 0.4 convolution_subtract_fusion.3
  175.8 0.5 convolution_subtract_fusion.5
  176.6 30.7 %all-gather.5.cloned.1.call-done = bf16[1024,512]{1,0:T(8,128)(2,1)} async-done(((bf16[64,512]{1,0:T(8,128)(2,1)}), bf16[1024,512]{1,0:T(8,128)(2,1)}) %all-gather.5.cloned.1.call-update) | async-done | bytes 1048592 | tf_op jit(solution)/shard_map/all_gather | solution.py:20
  207.3 2.4 %fusion = bf16[128,1024]{1,0:T(8,128)(2,1)} fusion(bf16[1024,512]{1,0:T(8,128)(2,1)} %all-gather.5.cloned.1.call-done, bf16[128,1024]{1,0:T(8,128)(2,1)S(1)} %copy-done.2, bf16[128,128]{1,0:T(8,128)(2,1)S(1)} %convolution_convert_fusion, bf16[128,128]{1,0:T(8,128)(2,1)S(1)} %get-tuple-element.34, bf16[128,128]{1,0:T(8,128)(2,1)S(1)} %get-tuple-element.36, ...), kind=kOutput, calls=%fused_computation.3 | convolution fusion | flops 135135232 | bytes 1703936 | tf_op jit(solution)/shard_map/dot_general | solution.py:21
  (44 shorter events, 5.1 us)
Async XLA Ops:
  7.2 26.4 %all-gather.3.cloned.1.call-start = ((), (), s32[]{:S(2)}) async-start(), calls=%async_computation | async-start | bytes 1572864 | tf_op jit(solution)/shard_map/all_gather | solution.py:8
  9.3 198.0 %all-gather.5.cloned.1.call-start = ((), (), s32[]{:S(2)}) async-start(), calls=%async_computation.1 | async-start | bytes 1114112 | tf_op jit(solution)/shard_map/all_gather | solution.py:20
  33.6 1.7 copy-start
  119.0 47.8 %copy-start.1 = (f32[64,512]{1,0:T(8,128)S(1)}, f32[64,512]{1,0:T(8,128)}, u32[]{:S(2)}) copy-start(f32[64,512]{1,0:T(8,128)} %param.4) | copy-start | bytes 393220
  175.8 31.5 %copy-start.2 = (bf16[128,1024]{1,0:T(8,128)(2,1)S(1)}, bf16[128,1024]{1,0:T(8,128)(2,1)}, u32[]{:S(2)}) copy-start(bf16[128,1024]{1,0:T(8,128)(2,1)} %param.5) | copy-start | bytes 786436
Sparse Core Ops, SparseCore 0:
  9.5 23.9 all-gather.2
  169.4 37.8 all-gather.4
where the time goes:
time: 217 us
  other arithmetic  119 us (55%)
  waiting for transfers between devices  54.9 us (25%)
  between operations  16.9 us (8%)
  local copies, waits for them, and re-layouts  12.3 us (6%)
  matrix products  8.2 us (4%)
  blocking collectives  4.93 us (2%)
    another operation x14, other arithmetic, per_device(): diag_factor = jnp.linalg.cholesky(tile_whole)  78.6 us
    another operation x3, other arithmetic, solve_rows(): jax.scipy.linalg.solve_triangular(diag_factor, panel_rows.T, lower=True)  39.7 us
    all_gather x1, waiting for transfers between devices, per_device(): block_low = lax.all_gather(low_panel, 'col', axis=0, tiled=True)  30.7 us
    all_gather x1, waiting for transfers between devices, per_device(): tile_whole = lax.all_gather(diagonal_tile, 'row', axis=0, tiled=True)  24.2 us
    another operation x12, local copies, waits for them, and re-layouts  8.39 us
    all_gather x1, blocking collectives, per_device(): lax.all_gather(panel.astype(jnp.bfloat16), 'row', axis=0, tiled=True)  4.93 us
  transfers between devices with their start and end apart: 2, of which 2 were waited for; matrix products, arithmetic and copies ran while one was open for 1% of the time, Pallas kernels for 0%

commit v1 on v0

v1 whole, which is shorter than its diff:
```python
import functools

import jax
import jax.numpy as jnp
from jax import lax
from jax.experimental import pallas as pl
from jax.experimental.pallas import tpu as pltpu
from jax.sharding import PartitionSpec as P

F32 = jnp.float32
BF16 = jnp.bfloat16
NB = 128
SUB = 8
BASE = 16
MESH = pl.DeviceIdType.MESH


def split2(x):
    hi = x.astype(BF16)
    return hi, (x - hi.astype(F32)).astype(BF16)


def dot3(a, b, dims):
    dims = (dims, ((), ()))
    a_hi, a_lo = split2(a)
    b_hi, b_lo = split2(b)
    dot = functools.partial(lax.dot_general, dimension_numbers=dims, preferred_element_type=F32)
    return dot(a_hi, b_hi) + (dot(a_hi, b_lo) + dot(a_lo, b_hi))


def dot_nt(a, b):
    return dot3(a, b, ((1,), (1,)))


def dot_nn(a, b):
    return dot3(a, b, ((1,), (0,)))


def row_of(x, s):
    return jnp.broadcast_to(x[s : s + 1, :], x.shape)


def lower_inverse(a):
    halves = BASE // SUB
    eye = (
        lax.broadcasted_iota(jnp.int32, (NB, NB), 0) == lax.broadcasted_iota(jnp.int32, (NB, NB), 1)
    ).astype(F32)
    iota = lax.broadcasted_iota(jnp.int32, (SUB, NB), 0)
    chunks = [
        (a[s : s + BASE, :], eye[s : s + BASE, :]) for s in range(0, NB, BASE)
    ]
    inverse_rows = []
    for kb in range(NB // BASE):
        cur = [
            [part[h * SUB : (h + 1) * SUB, :] for part in chunks[kb]] for h in range(halves)
        ]
        first = kb * BASE
        cols = [
            [
                jnp.broadcast_to(cur[h][0][:, first + c : first + c + 1], (SUB, NB))
                for h in range(halves)
            ]
            for c in range(BASE)
        ]
        scale = [jnp.zeros((SUB, NB), F32) for _ in range(halves)]
        for k in range(BASE):
            hk, sk = k // SUB, k % SUB
            root = lax.rsqrt(row_of(cols[k][hk], sk))
            inv = root * root
            scale[hk] = jnp.where(iota == sk, root, scale[hk])
            mult = {h: cols[k][h] * inv for h in range(hk, halves)}
            mult[hk] = jnp.where(iota > sk, mult[hk], 0.0)
            for c in range(k + 1, BASE):
                row = row_of(cols[c][hk], sk)
                for h in range(hk, halves):
                    cols[c][h] = cols[c][h] - mult[h] * row
            for part in range(2):
                row = row_of(cur[hk][part], sk)
                for h in range(hk, halves):
                    cur[h][part] = cur[h][part] - mult[h] * row
        done = [
            jnp.concatenate([cur[h][part] * scale[h] for h in range(halves)], axis=0)
            for part in range(2)
        ]
        inverse_rows.append(done[1])
        if kb + 1 < NB // BASE:
            pieces = []
            for part in range(2):
                hi = done[part].astype(BF16).astype(F32)
                pieces.append((hi, done[part] - hi))
            left = jnp.concatenate([pieces[0][0], pieces[0][0], pieces[0][1]], axis=0)
            left = left.T.astype(BF16)
            right = jnp.concatenate(
                [
                    jnp.concatenate([hi, lo, hi], axis=0) for hi, lo in pieces
                ],
                axis=1,
            ).astype(BF16)
            start = (kb + 1) * BASE
            change = lax.dot_general(
                left[start:, :], right, (((1,), (0,)), ((), ())), preferred_element_type=F32
            )
            for j in range(kb + 1, NB // BASE):
                at = j * BASE - start
                chunks[j] = tuple(
                    chunks[j][part] - change[at : at + BASE, part * NB : (part + 1) * NB]
                    for part in range(2)
                )
    return jnp.concatenate(inverse_rows, axis=0)


def kernel(
    n_row, n_col,
    tile_ref, panel_ref, trailing_ref,
    factor_ref, updated_ref,
    tile, rows, raw,
    tile_send, tile_recv, rows_send, rows_recv, raw_send, raw_recv,
):
    r = lax.axis_index("row")
    c = lax.axis_index("col")
    order = tile_ref.shape[1]
    blocks = order // NB
    per_dev = tile_ref.shape[0] // NB
    ch = panel_ref.shape[0]

    def row_peer(d):
        return (lax.rem(r + d, n_row), c)

    def col_peer(d):
        return (r, lax.rem(c + d, n_col))

    barrier = pltpu.get_barrier_semaphore()
    for d in range(1, n_row):
        pl.semaphore_signal(barrier, inc=1, device_id=row_peer(d), device_id_type=MESH)

    @pl.loop(1, n_col)
    def _(d):
        pl.semaphore_signal(barrier, inc=1, device_id=col_peer(d), device_id_type=MESH)

    own_raw = pl.ds(pl.multiple_of(c * ch, ch), ch)
    own_rows = pl.ds(pl.multiple_of(r * ch, ch), ch)
    raw[own_raw, :] = panel_ref[...].astype(BF16)
    rows[own_rows, :] = panel_ref[...]
    pl.semaphore_wait(barrier, n_row - 1 + n_col - 1)

    def tile_copy(i, d):
        source = pl.ds((i % per_dev) * NB, NB)
        cols = pl.ds(0, (i + 1) * NB)
        return pltpu.make_async_remote_copy(
            src_ref=tile_ref.at[source, cols],
            dst_ref=tile.at[pl.ds(i * NB, NB), cols],
            send_sem=tile_send.at[i, d - 1],
            recv_sem=tile_recv.at[i],
            device_id=row_peer(d),
            device_id_type=MESH,
        )

    def rows_copy(d):
        return pltpu.make_async_remote_copy(
            src_ref=panel_ref,
            dst_ref=rows.at[own_rows, :],
            send_sem=rows_send.at[d - 1],
            recv_sem=rows_recv.at[d - 1],
            device_id=row_peer(d),
            device_id_type=MESH,
        )

    def raw_copy(d):
        return pltpu.make_async_remote_copy(
            src_ref=raw.at[own_raw, :],
            dst_ref=raw.at[own_raw, :],
            send_sem=raw_send.at[d - 1],
            recv_sem=raw_recv.at[d - 1],
            device_id=col_peer(d),
            device_id_type=MESH,
        )

    for i in range(blocks):
        @pl.when(r == i // per_dev)
        def _():
            for d in range(1, n_row):
                tile_copy(i, d).start()
            here = (i % per_dev) * NB
            tile[i * NB : (i + 1) * NB, :] = tile_ref[here : here + NB, :]

    for d in range(1, n_row):
        rows_copy(d).start()

    @pl.loop(1, n_col)
    def _(d):
        raw_copy(d).start()

    def wait_tile(i):
        @pl.when(r != i // per_dev)
        def _():
            tile_copy(i, 1).wait_recv()

    def sl(i):
        return slice(i * NB, (i + 1) * NB)

    inverses = []
    for j in range(blocks):
        if j == 0:
            wait_tile(0)
        inv = lower_inverse(tile[sl(j), sl(j)])
        inverses.append(inv)
        if j == 0:
            for i in range(1, blocks):
                wait_tile(i)
            for d in range(1, n_row):
                rows_copy(d).wait_recv()
        solved = dot_nt(rows[:, sl(j)], inv)
        rows[:, sl(j)] = solved
        if j + 1 < blocks:
            lower = dot_nt(tile[(j + 1) * NB :, sl(j)], inv)
            tile[(j + 1) * NB :, sl(j)] = lower
            for k in range(j + 1, blocks):
                at = (k - j - 1) * NB
                pivot = lower[at : at + NB, :]
                tile[k * NB :, sl(k)] = tile[k * NB :, sl(k)] - dot_nt(lower[at:, :], pivot)
                rows[:, sl(k)] = rows[:, sl(k)] - dot_nt(solved, pivot)

    factor_ref[...] = rows[own_rows, :]
    weights = [None] * blocks
    for j in reversed(range(blocks)):
        value = rows[:, sl(j)]
        for i in range(j + 1, blocks):
            value = value - dot_nn(weights[i], tile[sl(i), sl(j)])
        weights[j] = dot_nn(value, inverses[j])
    weight = jnp.concatenate([w.astype(BF16) for w in weights], axis=1)

    @pl.loop(1, n_col)
    def _(d):
        raw_copy(d).wait_recv()

    wide = trailing_ref.shape[1]
    step = min(512, wide)
    for s in range(0, wide, step):
        term = lax.dot_general(
            weight, raw[s : s + step, :], (((1,), (1,)), ((), ())), preferred_element_type=F32
        )
        updated_ref[:, s : s + step] = (
            trailing_ref[:, s : s + step].astype(F32) - term
        ).astype(BF16)

    for i in range(blocks):
        @pl.when(r == i // per_dev)
        def _():
            for d in range(1, n_row):
                tile_copy(i, d).wait_send()
    for d in range(1, n_row):
        rows_copy(d).wait_send()

    @pl.loop(1, n_col)
    def _(d):
        raw_copy(d).wait_send()


def per_device(n_row, n_col, diagonal_tile, panel, trailing):
    order = diagonal_tile.shape[1]
    ch = panel.shape[0]
    dma = pltpu.SemaphoreType.DMA
    vmem = pl.BlockSpec(memory_space=pltpu.VMEM)
    return pl.pallas_call(
        functools.partial(kernel, n_row, n_col),
        out_shape=(
            jax.ShapeDtypeStruct(panel.shape, F32),
            jax.ShapeDtypeStruct(trailing.shape, BF16),
        ),
        in_specs=[vmem] * 3,
        out_specs=(vmem, vmem),
        scratch_shapes=[
            pltpu.VMEM((order, order), F32),
            pltpu.VMEM((n_row * ch, order), F32),
            pltpu.VMEM((n_col * ch, order), BF16),
            dma((order // NB, n_row - 1)),
            dma((order // NB,)),
            dma((n_row - 1,)),
            dma((n_row - 1,)),
            dma((n_col - 1,)),
            dma((n_col - 1,)),
        ],
        compiler_params=pltpu.CompilerParams(
            collective_id=0, has_side_effects=True, vmem_limit_bytes=48 * 1024 * 1024
        ),
    )(diagonal_tile, panel, trailing)


def solution(mesh):
    return jax.shard_map(
        functools.partial(per_device, mesh.shape["row"], mesh.shape["col"]),
        mesh=mesh,
        in_specs=(P("row", None), P(("row", "col"), None), P("col", "row")),
        out_specs=(P(("row", "col"), None), P("col", "row")),
        check_vma=False,
    )
```

time: 217 us -> 41.6 us (0.19)
  other arithmetic: 119 us -> 0 us
  waiting for transfers between devices: 54.9 us -> 0 us
  Pallas kernels: 0 us -> 36.5 us
  between operations: 16.9 us -> 0.65 us
  matrix products: 8.2 us -> 0 us
  local copies, waits for them, and re-layouts: 12.3 us -> 4.25 us
  blocking collectives: 4.93 us -> 0 us
    another operation x17 -> x0, other arithmetic: 118 us -> none  [the longest x14 78.6 us: per_device(): diag_factor = jnp.linalg.cholesky(tile_whole)]
    all_gather x2 -> x0, waiting for transfers between devices: 54.9 us -> none  [the longest x1 30.7 us: per_device(): block_low = lax.all_gather(low_panel, 'col', axis=0, tiled=True)]
    pallas_call x0 -> x1, Pallas kernels: none -> 36.5 us  [per_device(): pl.pallas_call(functools.partial(kernel, n_row, n_col), out_shape=(jax.Sh...]
    another operation x17 -> x0, local copies, waits for them, and re-layouts: 8.54 us -> none
    another operation x20 -> x0, matrix products: 5.79 us -> none  [the longest x14 3.93 us: solve_rows(): jax.scipy.linalg.solve_triangular(diag_factor, panel_rows.T, lower=True)]
    all_gather x1 -> x0, blocking collectives: 4.93 us -> none  [per_device(): lax.all_gather(panel.astype(jnp.bfloat16), 'row', axis=0, tiled=True)]
    dot_general x1 -> x0, matrix products: 2.41 us -> none  [per_device(): lax.dot_general(column_low, block_low, (((1,), (1,)), ((), ())), preferre...]
    unnamed x7 -> x8, local copies, waits for them, and re-layouts: 2.08 us -> 4.25 us
  transfers between devices with their start and end apart: 2 -> 0, of which waited for: 2 -> 0; matrix products, arithmetic and copies ran while one was open for 1% -> 0% of each run, Pallas kernels for 0% -> 0%
where the time goes in v1:
time: 41.6 us; the launch traced here: 41.4 us
  Pallas kernels  36.5 us (88%)
  local copies, waits for them, and re-layouts  4.25 us (10%)
  between operations  0.65 us (2%)
    pallas_call x1, Pallas kernels, per_device(): pl.pallas_call(functools.partial(kernel, n_row, n_col), out_shape=(jax.Sh...  36.5 us
    unnamed x8, local copies, waits for them, and re-layouts  4.25 us

profile of v1, /device:TPU:0, one launch (start us, length us, event | category | flops | bytes accessed | tf_op | source)
XLA Modules:
  0.0 41.4 jit_solution(13479966491724481190)
XLA Ops:
  0.6 0.0 copy-start
  0.6 1.0 %copy-done = f32[256,512]{1,0:T(8,128)S(1)} copy-done((f32[256,512]{1,0:T(8,128)S(1)}, f32[256,512]{1,0:T(8,128)}, u32[]{:S(2)}) %copy-start) | copy-done | bytes 524312
  1.7 0.0 copy-start.1
  1.7 0.9 %copy-done.1 = bf16[128,1024]{1,0:T(8,128)(2,1)S(1)} copy-done((bf16[128,1024]{1,0:T(8,128)(2,1)S(1)}, bf16[128,1024]{1,0:T(8,128)(2,1)}, u32[]{:S(2)}) %copy-start.1) | copy-done | bytes 262168
  2.6 0.0 copy-start.2
  2.6 0.9 %copy-done.2 = f32[64,512]{1,0:T(8,128)S(1)} copy-done((f32[64,512]{1,0:T(8,128)S(1)}, f32[64,512]{1,0:T(8,128)}, u32[]{:S(2)}) %copy-start.2) | copy-done | bytes 131096
  3.5 36.5 %shard_map.50 = (f32[64,512]{1,0:T(8,128)S(1)}, bf16[128,1024]{1,0:T(8,128)(2,1)S(1)}) custom-call(f32[256,512]{1,0:T(8,128)S(1)} %copy-done, f32[64,512]{1,0:T(8,128)S(1)} %copy-done.2, bf16[128,1024]{1,0:T(8,128)(2,1)S(1)} %copy-done.1), custom_call_target="tpu_custom_call" | custom-call | tf_op jit(solution)/shard_map/pallas_call | solution.py:264
  40.0 0.7 %copy.7 = f32[64,512]{1,0:T(8,128)} copy(f32[64,512]{1,0:T(8,128)S(1)} %get-tuple-element.4) | data formatting | bytes 262144
  40.7 0.7 %copy.8 = bf16[128,1024]{1,0:T(8,128)(2,1)} copy(bf16[128,1024]{1,0:T(8,128)(2,1)S(1)} %get-tuple-element.5) | data formatting | bytes 524288
Async XLA Ops:
  0.6 1.0 %copy-start = (f32[256,512]{1,0:T(8,128)S(1)}, f32[256,512]{1,0:T(8,128)}, u32[]{:S(2)}) copy-start(f32[256,512]{1,0:T(8,128)} %tile_ref.1) | copy-start | bytes 1572868
  1.7 0.9 %copy-start.1 = (bf16[128,1024]{1,0:T(8,128)(2,1)S(1)}, bf16[128,1024]{1,0:T(8,128)(2,1)}, u32[]{:S(2)}) copy-start(bf16[128,1024]{1,0:T(8,128)(2,1)} %trailing_ref.1) | copy-start | bytes 786436
  2.6 0.9 %copy-start.2 = (f32[64,512]{1,0:T(8,128)S(1)}, f32[64,512]{1,0:T(8,128)}, u32[]{:S(2)}) copy-start(f32[64,512]{1,0:T(8,128)} %panel_ref.1) | copy-start | bytes 393220

commit v2 on v1

--- a/solution.py
+++ b/solution.py
@@ -11,7 +11,7 @@
 BF16 = jnp.bfloat16
 NB = 128
 SUB = 8
-BASE = 16
+BASE = 32
 MESH = pl.DeviceIdType.MESH
 
 
@@ -40,41 +40,46 @@
     return jnp.broadcast_to(x[s : s + 1, :], x.shape)
 
 
-def lower_inverse(a):
+def lower_inverse(a, zero):
     halves = BASE // SUB
     eye = (
         lax.broadcasted_iota(jnp.int32, (NB, NB), 0) == lax.broadcasted_iota(jnp.int32, (NB, NB), 1)
     ).astype(F32)
     iota = lax.broadcasted_iota(jnp.int32, (SUB, NB), 0)
-    chunks = [
-        (a[s : s + BASE, :], eye[s : s + BASE, :]) for s in range(0, NB, BASE)
-    ]
+    chunks = [(a[s : s + BASE, :], eye[s : s + BASE, :]) for s in range(0, NB, BASE)]
     inverse_rows = []
     for kb in range(NB // BASE):
         cur = [
             [part[h * SUB : (h + 1) * SUB, :] for part in chunks[kb]] for h in range(halves)
         ]
         first = kb * BASE
+        last = kb + 1 == NB // BASE
+        parts = (1,) if last else (0, 1)
         cols = [
-            [
-                jnp.broadcast_to(cur[h][0][:, first + c : first + c + 1], (SUB, NB))
-                for h in range(halves)
-            ]
+            {
+                h: jnp.broadcast_to(cur[h][0][:, first + c : first + c + 1], (SUB, NB)) + zero
+                for h in range(c // SUB, halves)
+            }
             for c in range(BASE)
         ]
         scale = [jnp.zeros((SUB, NB), F32) for _ in range(halves)]
+        pivot = row_of(cols[0][0], 0)
         for k in range(BASE):
             hk, sk = k // SUB, k % SUB
-            root = lax.rsqrt(row_of(cols[k][hk], sk))
+            root = lax.rsqrt(pivot)
+            scale[hk] = jnp.where(iota == sk, root, scale[hk])
+            if k + 1 < BASE:
+                hn, sn = (k + 1) // SUB, (k + 1) % SUB
+                ahead = root * row_of(cols[k][hn], sn)
+                pivot = row_of(cols[k + 1][hn], sn) - ahead * ahead
             inv = root * root
-            scale[hk] = jnp.where(iota == sk, root, scale[hk])
             mult = {h: cols[k][h] * inv for h in range(hk, halves)}
             mult[hk] = jnp.where(iota > sk, mult[hk], 0.0)
             for c in range(k + 1, BASE):
-                row = row_of(cols[c][hk], sk)
-                for h in range(hk, halves):
+                row = row_of(cols[k][c // SUB], c % SUB)
+                for h in range(c // SUB, halves):
                     cols[c][h] = cols[c][h] - mult[h] * row
-            for part in range(2):
+            for part in parts:
                 row = row_of(cur[hk][part], sk)
                 for h in range(hk, halves):
                     cur[h][part] = cur[h][part] - mult[h] * row
@@ -83,7 +88,7 @@
             for part in range(2)
         ]
         inverse_rows.append(done[1])
-        if kb + 1 < NB // BASE:
+        if not last:
             pieces = []
             for part in range(2):
                 hi = done[part].astype(BF16).astype(F32)
@@ -91,10 +96,7 @@
             left = jnp.concatenate([pieces[0][0], pieces[0][0], pieces[0][1]], axis=0)
             left = left.T.astype(BF16)
             right = jnp.concatenate(
-                [
-                    jnp.concatenate([hi, lo, hi], axis=0) for hi, lo in pieces
-                ],
-                axis=1,
+                [jnp.concatenate([hi, lo, hi], axis=0) for hi, lo in pieces], axis=1
             ).astype(BF16)
             start = (kb + 1) * BASE
             change = lax.dot_general(
@@ -113,8 +115,9 @@
     n_row, n_col,
     tile_ref, panel_ref, trailing_ref,
     factor_ref, updated_ref,
-    tile, rows, raw,
-    tile_send, tile_recv, rows_send, rows_recv, raw_send, raw_recv,
+    tile, rows, raw, trail,
+    tile_local, panel_local, trail_local,
+    tile_send, tile_recv, rows_send, rows_recv, raw_send, raw_recv, pass_send, pass_recv,
 ):
     r = lax.axis_index("row")
     c = lax.axis_index("col")
@@ -126,26 +129,49 @@
     def row_peer(d):
         return (lax.rem(r + d, n_row), c)
 
+    half = n_col // 2
+    sibling = (r, c + 1 - 2 * lax.rem(c, 2))
+
     def col_peer(d):
-        return (r, lax.rem(c + d, n_col))
+        return (r, lax.rem(c + 2 * d, n_col))
 
     barrier = pltpu.get_barrier_semaphore()
     for d in range(1, n_row):
         pl.semaphore_signal(barrier, inc=1, device_id=row_peer(d), device_id_type=MESH)
 
-    @pl.loop(1, n_col)
+    pl.semaphore_signal(barrier, inc=1, device_id=sibling, device_id_type=MESH)
+
+    @pl.loop(1, half)
     def _(d):
         pl.semaphore_signal(barrier, inc=1, device_id=col_peer(d), device_id_type=MESH)
 
     own_raw = pl.ds(pl.multiple_of(c * ch, ch), ch)
     own_rows = pl.ds(pl.multiple_of(r * ch, ch), ch)
-    raw[own_raw, :] = panel_ref[...].astype(BF16)
-    rows[own_rows, :] = panel_ref[...]
-    pl.semaphore_wait(barrier, n_row - 1 + n_col - 1)
-
-    def tile_copy(i, d):
+    panel_in = pltpu.make_async_copy(panel_ref, rows.at[own_rows, :], panel_local)
+    panel_in.start()
+
+    def tile_in(i):
+        return pltpu.make_async_copy(
+            tile_ref.at[pl.ds((i % per_dev) * NB, NB), :],
+            tile.at[pl.ds(i * NB, NB), :],
+            tile_local.at[i],
+        )
+
+    for i in range(blocks):
+        @pl.when(r == i // per_dev)
+        def _():
+            tile_in(i).start()
+
+    trail_in = pltpu.make_async_copy(trailing_ref, trail, trail_local)
+    trail_in.start()
+    panel_in.wait()
+    raw[own_raw, :] = rows[own_rows, :].astype(BF16)
+    pl.semaphore_wait(barrier, n_row - 1 + half)
+
+    def tile_copy(i, d, target=None):
         source = pl.ds((i % per_dev) * NB, NB)
-        cols = pl.ds(0, (i + 1) * NB)
+        left = per_dev if target == 0 else 0
+        cols = pl.ds(left * NB, (i + 1 - left) * NB)
         return pltpu.make_async_remote_copy(
             src_ref=tile_ref.at[source, cols],
             dst_ref=tile.at[pl.ds(i * NB, NB), cols],
@@ -179,36 +205,65 @@
         @pl.when(r == i // per_dev)
         def _():
             for d in range(1, n_row):
-                tile_copy(i, d).start()
-            here = (i % per_dev) * NB
-            tile[i * NB : (i + 1) * NB, :] = tile_ref[here : here + NB, :]
+                tile_copy(i, d, (i // per_dev + d) % n_row).start()
 
     for d in range(1, n_row):
         rows_copy(d).start()
 
-    @pl.loop(1, n_col)
+    def pass_copy(d):
+        slot = pl.ds(pl.multiple_of(lax.rem(c + n_col - 2 * d, n_col) * ch, ch), ch)
+        return pltpu.make_async_remote_copy(
+            src_ref=raw.at[slot, :],
+            dst_ref=raw.at[slot, :],
+            send_sem=pass_send.at[d],
+            recv_sem=pass_recv.at[d],
+            device_id=sibling,
+            device_id_type=MESH,
+        )
+
+    @pl.loop(1, half)
     def _(d):
         raw_copy(d).start()
 
-    def wait_tile(i):
-        @pl.when(r != i // per_dev)
-        def _():
-            tile_copy(i, 1).wait_recv()
+    pass_copy(0).start()
 
     def sl(i):
         return slice(i * NB, (i + 1) * NB)
 
+    def wait_tile(i):
+        if i >= per_dev:
+            @pl.when(r == 0)
+            def _():
+                tile_copy(i, 1, 0).wait_recv()
+                for k in range(per_dev):
+                    tile[sl(i), sl(k)] = tile[sl(k), sl(i)].T
+
+        @pl.when((r != i // per_dev) & ((r != 0) | (i < per_dev)))
+        def _():
+            tile_copy(i, 1).wait_recv()
+
+        @pl.when(r == i // per_dev)
+        def _():
+            tile_in(i).wait()
+
+    zero = rows[pl.ds(pl.multiple_of(r * ch, ch), SUB), 0:NB] * 0.0
     inverses = []
     for j in range(blocks):
         if j == 0:
             wait_tile(0)
-        inv = lower_inverse(tile[sl(j), sl(j)])
+        inv = lower_inverse(tile[sl(j), sl(j)], zero)
         inverses.append(inv)
         if j == 0:
             for i in range(1, blocks):
                 wait_tile(i)
             for d in range(1, n_row):
                 rows_copy(d).wait_recv()
+        if j == min(1, blocks - 1):
+            @pl.loop(1, half)
+            def _(d):
+                raw_copy(d).wait_recv()
+                pass_copy(d).start()
+
         solved = dot_nt(rows[:, sl(j)], inv)
         rows[:, sl(j)] = solved
         if j + 1 < blocks:
@@ -229,10 +284,11 @@
         weights[j] = dot_nn(value, inverses[j])
     weight = jnp.concatenate([w.astype(BF16) for w in weights], axis=1)
 
-    @pl.loop(1, n_col)
-    def _(d):
-        raw_copy(d).wait_recv()
-
+    @pl.loop(0, half)
+    def _(d):
+        pass_copy(d).wait_recv()
+
+    trail_in.wait()
     wide = trailing_ref.shape[1]
     step = min(512, wide)
     for s in range(0, wide, step):
@@ -240,20 +296,24 @@
             weight, raw[s : s + step, :], (((1,), (1,)), ((), ())), preferred_element_type=F32
         )
         updated_ref[:, s : s + step] = (
-            trailing_ref[:, s : s + step].astype(F32) - term
+            trail[:, s : s + step].astype(F32) - term
         ).astype(BF16)
 
     for i in range(blocks):
         @pl.when(r == i // per_dev)
         def _():
             for d in range(1, n_row):
-                tile_copy(i, d).wait_send()
+                tile_copy(i, d, (i // per_dev + d) % n_row).wait_send()
     for d in range(1, n_row):
         rows_copy(d).wait_send()
 
-    @pl.loop(1, n_col)
+    @pl.loop(1, half)
     def _(d):
         raw_copy(d).wait_send()
+
+    @pl.loop(0, half)
+    def _(d):
+        pass_copy(d).wait_send()
 
 
 def per_device(n_row, n_col, diagonal_tile, panel, trailing):
@@ -267,21 +327,27 @@
             jax.ShapeDtypeStruct(panel.shape, F32),
             jax.ShapeDtypeStruct(trailing.shape, BF16),
         ),
-        in_specs=[vmem] * 3,
+        in_specs=[pl.BlockSpec(memory_space=pltpu.HBM)] * 3,
         out_specs=(vmem, vmem),
         scratch_shapes=[
             pltpu.VMEM((order, order), F32),
             pltpu.VMEM((n_row * ch, order), F32),
             pltpu.VMEM((n_col * ch, order), BF16),
+            pltpu.VMEM(trailing.shape, BF16),
+            dma((order // NB,)),
+            dma,
+            dma,
             dma((order // NB, n_row - 1)),
             dma((order // NB,)),
             dma((n_row - 1,)),
             dma((n_row - 1,)),
-            dma((n_col - 1,)),
-            dma((n_col - 1,)),
+            dma((n_col // 2 - 1,)),
+            dma((n_col // 2 - 1,)),
+            dma((n_col // 2,)),
+            dma((n_col // 2,)),
         ],
         compiler_params=pltpu.CompilerParams(
-            collective_id=0, has_side_effects=True, vmem_limit_bytes=48 * 1024 * 1024
+            collective_id=0, has_side_effects=True, vmem_limit_bytes=67_000_000
         ),
     )(diagonal_tile, panel, trailing)
 

time: 41.6 us -> 31.6 us (0.76)
  Pallas kernels: 36.5 us -> 28.5 us
  local copies, waits for them, and re-layouts: 4.25 us -> 2.32 us
    pallas_call x1, Pallas kernels: 36.5 us -> 28.5 us  [per_device(): pl.pallas_call(functools.partial(kernel, n_row, n_col), out_shape=(jax.Sh...]
    unnamed x8 -> x4, local copies, waits for them, and re-layouts: 4.25 us -> 2.32 us
where the time goes in v2:
time: 31.6 us; the launch traced here: 31.5 us
  Pallas kernels  28.5 us (90%)
  local copies, waits for them, and re-layouts  2.32 us (7%)
  between operations  0.65 us (2%)
    pallas_call x1, Pallas kernels, per_device(): pl.pallas_call(functools.partial(kernel, n_row, n_col), out_shape=(jax.Sh...  28.5 us
    unnamed x4, local copies, waits for them, and re-layouts  2.32 us

profile of v2, /device:TPU:0, one launch (start us, length us, event | category | flops | bytes accessed | tf_op | source)
XLA Modules:
  0.0 31.5 jit_solution(8686982047492901516)
XLA Ops:
  0.6 28.5 %shard_map.50 = (f32[64,512]{1,0:T(8,128)}, bf16[128,1024]{1,0:T(8,128)(2,1)}) custom-call(f32[256,512]{1,0:T(8,128)} %tile_ref.1, f32[64,512]{1,0:T(8,128)} %panel_ref.1, bf16[128,1024]{1,0:T(8,128)(2,1)} %trailing_ref.1), custom_call_target="tpu_custom_call" | custom-call | tf_op jit(solution)/shard_map/pallas_call | solution.py:324
  29.1 0.0 copy-start
  29.1 1.6 %copy.7 = f32[64,512]{1,0:T(8,128)} copy(f32[64,512]{1,0:T(8,128)} %get-tuple-element.4) | data formatting | bytes 262144
  30.8 0.0 copy-done
  30.8 0.7 %copy.8 = bf16[128,1024]{1,0:T(8,128)(2,1)} copy(bf16[128,1024]{1,0:T(8,128)(2,1)S(1)} %copy-done) | data formatting | bytes 524288
Async XLA Ops:
  29.1 1.6 %copy-start = (bf16[128,1024]{1,0:T(8,128)(2,1)S(1)}, bf16[128,1024]{1,0:T(8,128)(2,1)}, u32[]{:S(2)}) copy-start(bf16[128,1024]{1,0:T(8,128)(2,1)} %get-tuple-element.5) | copy-start | bytes 786436

commit v3 on v2

--- a/solution.py
+++ b/solution.py
@@ -115,7 +115,7 @@
     n_row, n_col,
     tile_ref, panel_ref, trailing_ref,
     factor_ref, updated_ref,
-    tile, rows, raw, trail,
+    tile, rows, raw, trail, full,
     tile_local, panel_local, trail_local,
     tile_send, tile_recv, rows_send, rows_recv, raw_send, raw_recv, pass_send, pass_recv,
 ):
@@ -247,12 +247,14 @@
             tile_in(i).wait()
 
     zero = rows[pl.ds(pl.multiple_of(r * ch, ch), SUB), 0:NB] * 0.0
-    inverses = []
+    full[...] = jnp.zeros_like(full)
+    weights = [None] * blocks
     for j in range(blocks):
         if j == 0:
             wait_tile(0)
+        done = j * NB
+        coupling = dot_nn(tile[sl(j), :done], full[:done, :done]) if j else None
         inv = lower_inverse(tile[sl(j), sl(j)], zero)
-        inverses.append(inv)
         if j == 0:
             for i in range(1, blocks):
                 wait_tile(i)
@@ -266,6 +268,13 @@
 
         solved = dot_nt(rows[:, sl(j)], inv)
         rows[:, sl(j)] = solved
+        inverse_row = inv
+        if j:
+            inverse_row = jnp.concatenate([-dot_nn(inv, coupling), inv], axis=1)
+        full[sl(j), : done + NB] = inverse_row
+        term = dot_nn(solved, inverse_row)
+        for k in range(j + 1):
+            weights[k] = term[:, sl(k)] if k == j else weights[k] + term[:, sl(k)]
         if j + 1 < blocks:
             lower = dot_nt(tile[(j + 1) * NB :, sl(j)], inv)
             tile[(j + 1) * NB :, sl(j)] = lower
@@ -276,12 +285,6 @@
                 rows[:, sl(k)] = rows[:, sl(k)] - dot_nt(solved, pivot)
 
     factor_ref[...] = rows[own_rows, :]
-    weights = [None] * blocks
-    for j in reversed(range(blocks)):
-        value = rows[:, sl(j)]
-        for i in range(j + 1, blocks):
-            value = value - dot_nn(weights[i], tile[sl(i), sl(j)])
-        weights[j] = dot_nn(value, inverses[j])
     weight = jnp.concatenate([w.astype(BF16) for w in weights], axis=1)
 
     @pl.loop(0, half)
@@ -334,6 +337,7 @@
             pltpu.VMEM((n_row * ch, order), F32),
             pltpu.VMEM((n_col * ch, order), BF16),
             pltpu.VMEM(trailing.shape, BF16),
+            pltpu.VMEM((order, order), F32),
             dma((order // NB,)),
             dma,
             dma,

time: 31.6 us -> 31.4 us (level)
  no operation moved by 1% of the time
where the time goes in v3:
time: 31.4 us; the launch traced here: 31.3 us
  Pallas kernels  28.3 us (90%)
  local copies, waits for them, and re-layouts  2.32 us (7%)
  between operations  0.65 us (2%)
    pallas_call x1, Pallas kernels, per_device(): pl.pallas_call(functools.partial(kernel, n_row, n_col), out_shape=(jax.Sh...  28.3 us
    unnamed x4, local copies, waits for them, and re-layouts  2.32 us

profile of v3, /device:TPU:0, one launch (start us, length us, event | category | flops | bytes accessed | tf_op | source)
XLA Modules:
  0.0 31.3 jit_solution(10254269010181009813)
XLA Ops:
  0.6 28.3 %shard_map.50 = (f32[64,512]{1,0:T(8,128)}, bf16[128,1024]{1,0:T(8,128)(2,1)}) custom-call(f32[256,512]{1,0:T(8,128)} %tile_ref.1, f32[64,512]{1,0:T(8,128)} %panel_ref.1, bf16[128,1024]{1,0:T(8,128)(2,1)} %trailing_ref.1), custom_call_target="tpu_custom_call" | custom-call | tf_op jit(solution)/shard_map/pallas_call | solution.py:327
  29.0 0.0 copy-start
  29.0 1.6 %copy.7 = f32[64,512]{1,0:T(8,128)} copy(f32[64,512]{1,0:T(8,128)} %get-tuple-element.4) | data formatting | bytes 262144
  30.6 0.0 copy-done
  30.6 0.7 %copy.8 = bf16[128,1024]{1,0:T(8,128)(2,1)} copy(bf16[128,1024]{1,0:T(8,128)(2,1)S(1)} %copy-done) | data formatting | bytes 524288
Async XLA Ops:
  29.0 1.6 %copy-start = (bf16[128,1024]{1,0:T(8,128)(2,1)S(1)}, bf16[128,1024]{1,0:T(8,128)(2,1)}, u32[]{:S(2)}) copy-start(bf16[128,1024]{1,0:T(8,128)(2,1)} %get-tuple-element.5) | copy-start | bytes 786436
